TPU v7x, 32 devices: a whole 2x2x4 slice. The times are simulated.
32 devices in a mesh: section: 4 (over x, core), seq: 8 (over z, y).
Axes of the slice: x: 2, y: 2, z: 4, core: 2. Of those that a mesh axis runs over, the one named last changes fastest.
Arguments:
- layer_input: bfloat16 [4, 512, 4, 1536], P('section', 'seq'), may hold values from -300 to 300
- norm_gain: float32 [4, 1536], P('section'), may hold values from 0.1 to 1.9
- queries: bfloat16 [4, 512, 4, 1024], P('section', 'seq'), may hold values from -6 to 6
- key_states: bfloat16 [4, 512, 4, 1024], P('section', 'seq'), may hold values from -6 to 6
- value_states: bfloat16 [4, 512, 4, 1024], P('section', 'seq'), may hold values from -6 to 6
- out_grad: bfloat16 [4, 512, 4, 1536], P('section', 'seq'), may hold values from -6 to 6
- out_weight: bfloat16 [4, 1024, 1536], P('section', 'seq'), may hold values from -0.1875 to 0.1875
- qkv_weight: bfloat16 [4, 1536, 3072], P('section', 'seq'), may hold values from -0.15625 to 0.15625
- lengths: int32 [4, 4], P('section'), may hold values from 256 to 512
Outputs:
- passed_grad: bfloat16 [4, 512, 4, 1536], P('section', 'seq')
All inputs are finite; a program needn't handle non-finite values.
Results may differ from a plain program's by a relative error of at most 0.0034.
Values may be sent and summed in bfloat16 or wider, within the bound.
A program may use at most 128 MiB of HBM per device.

v0:
```python
import functools

import jax
import jax.numpy as jnp
from jax import lax
from jax.experimental import pallas as pl
from jax.experimental.pallas import tpu as pltpu
from jax.sharding import PartitionSpec as P

HEADS = 16
HS = 64


EPSILON = 1e-05
MASKED = -1e30
ROW_DOT = (((1,), (1,)), ((), ()))
COL_DOT = (((0,), (0,)), ((), ()))


def shifted(shard, axis, by):
    count = lax.axis_size(axis)
    return lax.ppermute(shard, axis, [(i, (i + by) % count) for i in range(count)])


def item_backward(query_rows, key_rows, value_rows, grad_rows, key_valid):
    length = query_rows.shape[0]
    block = min(512, length)
    scale = HS ** (-0.5)
    offsets = jnp.arange(0, length, block)
    zeros = jnp.zeros((length, query_rows.shape[1]), jnp.float32)

    def step(carry, offset):
        key_total, value_total = carry
        query_block = lax.dynamic_slice_in_dim(query_rows, offset, block, 0)
        grad_block = lax.dynamic_slice_in_dim(grad_rows, offset, block, 0)
        scores = (
            lax.dot_general(query_block, key_rows, ROW_DOT, preferred_element_type=jnp.float32)
            * scale
        )
        scores = jnp.where(key_valid[None, :], scores, MASKED)
        largest = jnp.max(scores, axis=1, keepdims=True)
        weights = jnp.exp(scores - largest)
        probs = weights / jnp.sum(weights, axis=1, keepdims=True)
        probs_low = probs.astype(jnp.bfloat16)
        grad_probs = lax.dot_general(
            grad_block, value_rows, ROW_DOT, preferred_element_type=jnp.float32
        )
        centre = jnp.sum(probs * grad_probs, axis=1, keepdims=True)
        grad_scores = (probs * (grad_probs - centre) * scale).astype(jnp.bfloat16)
        query_grad = jnp.dot(grad_scores, key_rows, preferred_element_type=jnp.float32)
        key_total = key_total + lax.dot_general(
            grad_scores, query_block, COL_DOT, preferred_element_type=jnp.float32
        )
        value_total = value_total + lax.dot_general(
            probs_low, grad_block, COL_DOT, preferred_element_type=jnp.float32
        )
        return ((key_total, value_total), query_grad.astype(jnp.bfloat16))

    (key_total, value_total), query_parts = lax.scan(step, (zeros, zeros), offsets)
    query_grad = query_parts.reshape(length, query_rows.shape[1])
    return (query_grad, key_total.astype(jnp.bfloat16), value_total.astype(jnp.bfloat16))


def split_items(columns):
    length = columns.shape[0]
    count = columns.shape[1] // HS
    return columns.reshape(length, count, HS).transpose(1, 0, 2)


def join_items(items):
    count = items.shape[0]
    length = items.shape[1]
    return items.transpose(1, 0, 2).reshape(length, count * HS)


def project_grad(flat_grad, out_rows):
    return lax.dot_general(
        flat_grad,
        lax.all_gather(out_rows, "seq", axis=0, tiled=True),
        ROW_DOT,
        preferred_element_type=jnp.float32,
    ).astype(jnp.bfloat16)


def on_device(
    layer_input,
    norm_gain,
    queries,
    key_states,
    value_states,
    out_grad,
    out_weight,
    qkv_weight,
    lengths,
):
    frames = queries.shape[1]
    records = queries.shape[2]
    features = queries.shape[3]
    model_width = out_grad.shape[3]
    flat_grad = out_grad[0].reshape(frames * records, model_width)
    frame_queries = queries[0].reshape(frames, records * features)
    frame_keys = key_states[0].reshape(frames, records * features)
    frame_values = value_states[0].reshape(frames, records * features)
    attn_grad = project_grad(flat_grad, out_weight[0])
    head_queries, head_keys, head_values, head_grads = (
        lax.all_to_all(frame_queries, "seq", split_axis=1, concat_axis=0, tiled=True),
        lax.all_to_all(frame_keys, "seq", split_axis=1, concat_axis=0, tiled=True),
        lax.all_to_all(frame_values, "seq", split_axis=1, concat_axis=0, tiled=True),
        lax.all_to_all(
            attn_grad.reshape(frames, records * features),
            "seq",
            split_axis=1,
            concat_axis=0,
            tiled=True,
        ),
    )
    items_here = head_queries.shape[1] // HS
    length = head_queries.shape[0]
    item_ids = lax.axis_index("seq") * items_here + jnp.arange(items_here, dtype=jnp.int32)
    record_ids = item_ids // HEADS
    record_pick = jnp.arange(records, dtype=jnp.int32)[None, :] == record_ids[:, None]
    item_lengths = jnp.sum(jnp.where(record_pick, lengths[0][None, :], 0), axis=1)
    key_valid = jnp.arange(length, dtype=jnp.int32)[None, :] < item_lengths[:, None]
    query_grad, key_gradient, value_grad = lax.map(
        lambda group: item_backward(*group),
        (
            split_items(head_queries),
            split_items(head_keys),
            split_items(head_values),
            split_items(head_grads),
            key_valid,
        ),
    )
    query_back, key_backward, value_back = (
        lax.all_to_all(join_items(query_grad), "seq", split_axis=0, concat_axis=1, tiled=True),
        lax.all_to_all(join_items(key_gradient), "seq", split_axis=0, concat_axis=1, tiled=True),
        lax.all_to_all(join_items(value_grad), "seq", split_axis=0, concat_axis=1, tiled=True),
    )
    joined = jnp.concatenate(
        [
            query_back.reshape(frames * records, features),
            key_backward.reshape(frames * records, features),
            value_back.reshape(frames * records, features),
        ],
        axis=1,
    )
    norm_grad = lax.dot_general(
        joined,
        lax.all_gather(qkv_weight[0], "seq", axis=0, tiled=True),
        ROW_DOT,
        preferred_element_type=jnp.float32,
    )
    inputs = layer_input[0].reshape(frames * records, model_width).astype(jnp.float32)
    row_average = jnp.mean(inputs, axis=1, keepdims=True)
    centered_input = inputs - row_average
    var = jnp.mean(centered_input * centered_input, axis=1, keepdims=True)
    inverse_deviation = 1.0 / jnp.sqrt(var + EPSILON)
    normalized_input = centered_input * inverse_deviation
    scaled_rows = norm_grad * norm_gain[0][None, :]
    residual_branch = inverse_deviation * (
        scaled_rows
        - jnp.mean(scaled_rows, axis=1, keepdims=True)
        - normalized_input * jnp.mean(scaled_rows * normalized_input, axis=1, keepdims=True)
    )
    input_grad = (flat_grad.astype(jnp.float32) + residual_branch).astype(jnp.bfloat16)
    input_grad = input_grad.reshape(1, frames, records, model_width)
    return shifted(input_grad, "section", -1)


def body(
    dims,
    length_ref,
    li_ref,
    q_ref,
    k_ref,
    v_ref,
    og_ref,
    ow_in,
    w_in,
    gain_ref,
    out_ref,
    xq,
    xk,
    xv,
    xg,
    g_send,
    ow,
    w,
    joined,
    part_send,
    side_recv,
    sum_send,
    part_recv,
    li_here,
    og_here,
    x_send_sem,
    x_recv_sem,
    ow_send_sem,
    ow_side_sem,
    ow_recv_sem,
    w_send_sem,
    w_side_sem,
    w_near_sem,
    w_recv_sem,
    side_send_sem,
    side_recv_sem,
    p_send_sem,
    p_recv_sem,
    s_send_sem,
    s_recv_sem,
    local_sem,
):
    n, sections, groups, parts, frames, cols = dims
    pairs = cols // (2 * HS)
    section = lax.axis_index("section")
    me = lax.axis_index("seq")
    group = me // parts
    part = me % parts
    before = (section + sections - 1) % sections
    after = (section + 1) % sections

    def remote(src, dst, send, recv, sec, dev):
        return pltpu.make_async_remote_copy(
            src_ref=src,
            dst_ref=dst,
            send_sem=send,
            recv_sem=recv,
            device_id=(sec, dev),
            device_id_type=pl.DeviceIdType.MESH,
        )

    barrier = pltpu.get_barrier_semaphore()

    def greet(sec, dev):
        pl.semaphore_signal(
            barrier, inc=1, device_id=(sec, dev), device_id_type=pl.DeviceIdType.MESH
        )

    for k in range(1, n):
        greet(section, (me + k) % n)
    for k in range(n):
        greet(before, (me + k) % n)
        greet(after, (me + k) % n)

    heads = [(q_ref, xq), (k_ref, xk), (v_ref, xv), (g_send, xg)]

    def own(t):
        src, dst = heads[t]
        return pltpu.make_async_copy(
            src.at[group, :, pl.ds(pl.multiple_of(part * cols, cols), cols)],
            dst.at[me],
            local_sem.at[t],
        )

    def exchange(t, k):
        src, dst = heads[t]
        to = (me + k) % n
        return remote(
            src.at[to // parts, :, pl.ds(pl.multiple_of((to % parts) * cols, cols), cols)],
            dst.at[me],
            x_send_sem.at[t, k],
            x_recv_sem.at[t, k],
            section,
            to,
        )

    local_ow = pltpu.make_async_copy(ow_in, ow.at[me], local_sem.at[4])

    def piece(t, which):
        return w_in.at[:, pl.ds(pl.multiple_of((t * parts + which) * cols, cols), cols)]

    def local_w(t):
        return pltpu.make_async_copy(
            piece(t, part), w.at[me, :, pl.ds(t * cols, cols)], local_sem.at[5 + t]
        )

    local_ow.start()
    for t in range(3):
        local_w(t).start()
    for t in range(3):
        own(t).start()
    pl.semaphore_wait(barrier, 3 * n - 1)
    local_ow.wait()

    def ow_hop(slot, way, dev):
        return remote(
            ow.at[slot], ow.at[slot], ow_send_sem.at[way, slot], ow_recv_sem.at[slot], section, dev
        )

    def ow_side(slot, k):
        return remote(
            ow.at[slot],
            ow.at[slot],
            ow_side_sem.at[k, slot],
            ow_recv_sem.at[slot],
            section,
            group * parts + (part + k) % parts,
        )

    def w_hop(slot, way, dev):
        return remote(
            w.at[slot], w.at[slot], w_send_sem.at[way, slot], w_recv_sem.at[slot], section, dev
        )

    def w_side(t, k):
        other = (part + k) % parts
        return remote(
            piece(t, other),
            w.at[me, :, pl.ds(t * cols, cols)],
            w_side_sem.at[t, k],
            w_near_sem.at[t, k],
            section,
            group * parts + other,
        )

    def ways(origin, act):
        @pl.when((origin <= group) & (group + 1 < groups))
        def _():
            act(0, me + parts)

        @pl.when((origin >= group) & (group >= 1))
        def _():
            act(1, me - parts)

    def ow_pass(origin):
        slot = origin * parts + part
        ways(origin, lambda way, dev: ow_hop(slot, way, dev).start())
        for k in range(1, parts):
            ow_side(slot, k).start()

    def ow_arrive(origin):
        @pl.when((origin >= 0) & (origin < groups))
        def _():
            slot = origin * parts + part
            ow_hop(slot, 0, me).wait_recv()
            ow_pass(origin)

    def w_pass(origin):
        @pl.when((origin >= 0) & (origin < groups))
        def _():
            for other in range(parts):
                slot = origin * parts + other
                w_hop(slot, 0, me).wait_recv()
                ways(origin, lambda way, dev: w_hop(slot, way, dev).start())

    def w_first():
        for t in range(3):
            local_w(t).wait()
        ways(group, lambda way, dev: w_hop(me, way, dev).start())
        for k in range(1, parts):
            for t in range(3):
                w_side(t, k).wait_recv()
            slot = group * parts + (part + parts - k) % parts
            ways(group, lambda way, dev: w_hop(slot, way, dev).start())

    ow_pass(group)
    shift_og = remote(og_ref, og_here, s_send_sem.at[0], s_recv_sem.at[0], before, me)
    shift_li = remote(li_ref, li_here, s_send_sem.at[1], s_recv_sem.at[1], before, me)
    for k in range(1, n):
        exchange(0, k).start()
    shift_og.start()
    shift_li.start()
    for s in range(1, groups):
        ow_arrive(group - s)
        ow_arrive(group + s)
    for k in range(1, parts):
        for t in range(3):
            w_side(t, k).start()
    for t in (1, 2):
        for k in range(1, n):
            exchange(t, k).start()
    w_first()
    for origin in range(groups):
        for k in range(1, parts):
            ow_side(origin * parts + (part + k) % parts, k).wait_recv()

    features = groups * parts
    rows_here = ow.shape[1]

    def project(i, carry):
        weight = ow[pl.ds(2 * i, 2)].reshape(2 * rows_here, ow.shape[2])
        result = lax.dot_general(
            og_ref[...], weight, ROW_DOT, preferred_element_type=jnp.float32
        ).astype(jnp.bfloat16)
        g_send[:, :, pl.ds(pl.multiple_of(i * 2 * rows_here, 2 * rows_here), 2 * rows_here)] = (
            result.reshape(groups, frames, 2 * rows_here)
        )
        return carry

    lax.fori_loop(0, features // 2, project, 0)
    own(3).start()
    for k in range(1, n):
        exchange(3, k).start()
    w_pass(group - 1)
    w_pass(group + 1)
    for t in range(4):
        own(t).wait()
        for k in range(1, n):
            exchange(t, k).wait_recv()

    length = n * frames
    valid = length_ref[0]
    keys_ok = lax.broadcasted_iota(jnp.int32, (length, 1), 0) < valid
    low_lanes = lax.broadcasted_iota(jnp.int32, (length, 2 * HS), 1) < HS
    scale = HS ** (-0.5)

    def attend(j, carry):
        lanes = pl.ds(pl.multiple_of(j * 2 * HS, 2 * HS), 2 * HS)
        queries, keys, values, grads = (
            x[:, :, lanes].reshape(length, 2 * HS) for x in (xq, xk, xv, xg)
        )
        keys_across = keys.T
        nothing = jnp.zeros_like(keys)
        halves = []
        for h in range(2):
            mine = low_lanes if h == 0 else jnp.logical_not(low_lanes)
            key_h = jnp.where(mine, keys, nothing)
            value_h = jnp.where(mine, values, nothing)
            scores = (
                lax.dot_general(key_h, queries, ROW_DOT, preferred_element_type=jnp.float32)
                * scale
            )
            scores = jnp.where(keys_ok, scores, MASKED)
            weights = jnp.exp(scores - jnp.max(scores, axis=0, keepdims=True))
            probs = weights * (1.0 / jnp.sum(weights, axis=0, keepdims=True))
            grad_probs = lax.dot_general(
                value_h, grads, ROW_DOT, preferred_element_type=jnp.float32
            )
            centre = jnp.sum(probs * grad_probs, axis=0, keepdims=True)
            grad_scores = (probs * (grad_probs - centre)).astype(jnp.bfloat16)
            value_grad = jnp.dot(
                probs.astype(jnp.bfloat16), grads, preferred_element_type=jnp.float32
            )
            key_grad = jnp.dot(grad_scores, queries, preferred_element_type=jnp.float32)
            query_grad = jnp.dot(
                keys_across[h * HS : (h + 1) * HS], grad_scores, preferred_element_type=jnp.float32
            )
            halves.append((query_grad, key_grad, value_grad))
        (query_0, key_0, value_0), (query_1, key_1, value_1) = halves
        query_both = (jnp.concatenate([query_0, query_1], axis=0) * scale).T
        key_both = jnp.where(low_lanes, key_0, key_1) * scale
        value_both = jnp.where(low_lanes, value_0, value_1)
        for t, both in enumerate((query_both, key_both, value_both)):
            at = pl.multiple_of(t * cols + j * 2 * HS, 2 * HS)
            joined[:, pl.ds(at, 2 * HS)] = both.astype(jnp.bfloat16)

        @pl.when(j == pairs - 2)
        def _():
            w_pass(group - 2)
            w_pass(group + 2)

        return carry

    if pairs < 2:
        w_pass(group - 2)
        w_pass(group + 2)
    lax.fori_loop(0, pairs, attend, 0)

    def side_copy(origin, k):
        other = (part + k) % parts
        return remote(
            part_send.at[origin, other],
            side_recv.at[origin, k],
            side_send_sem.at[origin, k],
            side_recv_sem.at[origin, k],
            section,
            group * parts + other,
        )

    def sum_copy(origin, to):
        return remote(
            sum_send.at[origin, to],
            part_recv.at[group, origin],
            p_send_sem.at[origin, to],
            p_recv_sem.at[group, origin],
            before,
            to * parts + part,
        )

    blocks = 2 * groups - 1

    def origin_of(i):
        return group + ((i + 1) // 2) * (1 - 2 * (i % 2))

    def norm_block(i, carry):
        earlier = origin_of(i - 2)

        @pl.when((i >= 2) & (earlier >= 0) & (earlier < groups))
        def _():
            total = part_send[earlier, part].astype(jnp.float32)
            for k in range(1, parts):
                side_copy(earlier, k).wait_recv()
                total = total + side_recv[earlier, k].astype(jnp.float32)
            sum_send[earlier] = total.astype(jnp.bfloat16)
            for k in range(groups):
                sum_copy(earlier, (group + k) % groups).start()

        origin = origin_of(i)

        @pl.when((i >= 5) & (i < blocks))
        def _():
            w_pass(origin)

        @pl.when((i < blocks) & (origin >= 0) & (origin < groups))
        def _():
            weight = w[pl.ds(origin * parts, parts)].reshape(parts * w.shape[1], w.shape[2])
            sums = lax.dot_general(
                joined[...], weight, ROW_DOT, preferred_element_type=jnp.float32
            )
            sums = (sums * gain_ref[origin]).astype(jnp.bfloat16)
            sums = sums.reshape(groups, parts, frames, sums.shape[1])
            for other in range(parts):
                part_send[origin, other] = sums[:, other]
            for k in range(1, parts):
                side_copy(origin, k).start()

        return carry

    lax.fori_loop(0, blocks + 2, norm_block, 0)

    shift_og.wait_recv()
    shift_li.wait_recv()
    for src in range(groups):
        for origin in range(groups):
            remote(
                sum_send.at[origin, 0],
                part_recv.at[src, origin],
                p_send_sem.at[origin, 0],
                p_recv_sem.at[src, origin],
                before,
                me,
            ).wait_recv()

    width = og_here.shape[1]

    def finish(r):
        rows = pl.ds(r * frames, frames)
        inputs = li_here[:, r, :].astype(jnp.float32)
        centered = inputs - jnp.sum(inputs, axis=1, keepdims=True) * (1.0 / width)
        var = jnp.sum(centered * centered, axis=1, keepdims=True) * (1.0 / width)
        deviation = 1.0 / jnp.sqrt(var + EPSILON)
        normal = centered * deviation
        scaled = []
        for origin in range(groups):
            scaled.append(part_recv[r, origin].astype(jnp.float32))
        scaled = jnp.concatenate(scaled, axis=1)
        average = jnp.sum(scaled, axis=1, keepdims=True) * (1.0 / width)
        along = jnp.sum(scaled * normal, axis=1, keepdims=True) * (1.0 / width)
        branch = deviation * (scaled - average - normal * along)
        out_ref[rows, :] = (og_here[rows, :].astype(jnp.float32) + branch).astype(jnp.bfloat16)

    for r in range(groups):
        finish(r)

    for t in range(4):
        for k in range(1, n):
            exchange(t, k).wait_send()
    for origin in range(groups):
        slot = origin * parts + part
        ways(origin, lambda way, dev: ow_hop(slot, way, dev).wait_send())
        for k in range(1, parts):
            ow_side(slot, k).wait_send()
        for other in range(parts):
            w_slot = origin * parts + other
            ways(origin, lambda way, dev: w_hop(w_slot, way, dev).wait_send())
        for to in range(groups):
            sum_copy(origin, to).wait_send()
        for k in range(1, parts):
            side_copy(origin, k).wait_send()
    for k in range(1, parts):
        for t in range(3):
            w_side(t, k).wait_send()
    shift_og.wait_send()
    shift_li.wait_send()


def on_device_fused(
    layer_input,
    norm_gain,
    queries,
    key_states,
    value_states,
    out_grad,
    out_weight,
    qkv_weight,
    lengths,
):
    n = lax.axis_size("seq")
    sections = lax.axis_size("section")
    frames, records, features = queries.shape[1:]
    width = out_grad.shape[3]
    parts = n // records
    cols = features // parts
    ow_rows = out_weight.shape[1]
    w_rows = qkv_weight.shape[1]
    block = parts * w_rows
    group = lax.axis_index("seq") // parts
    length_here = lax.dynamic_slice(lengths[0], (group,), (1,))

    def by_record(x):
        return x[0].transpose(1, 0, 2)

    flat_input = layer_input[0]
    flat_grad = by_record(out_grad).reshape(records * frames, width)
    gain = norm_gain[0].reshape(records, 1, block)
    vmem = pl.BlockSpec(memory_space=pltpu.VMEM)
    low = jnp.bfloat16
    dma = pltpu.SemaphoreType.DMA
    out = pl.pallas_call(
        functools.partial(body, (n, sections, records, parts, frames, cols)),
        out_shape=jax.ShapeDtypeStruct((records * frames, width), low),
        in_specs=[pl.BlockSpec(memory_space=pltpu.SMEM)] + [vmem] * 8,
        out_specs=vmem,
        scratch_shapes=[pltpu.VMEM((n, frames, cols), low)] * 4
        + [
            pltpu.VMEM((records, frames, features), low),
            pltpu.VMEM((n, ow_rows, width), low),
            pltpu.VMEM((n, w_rows, 3 * cols), low),
            pltpu.VMEM((n * frames, 3 * cols), low),
            pltpu.VMEM((records, parts, records, frames, block), low),
            pltpu.VMEM((records, parts, records, frames, block), low),
            pltpu.VMEM((records, records, frames, block), low),
            pltpu.VMEM((records, records, frames, block), low),
            pltpu.VMEM((frames, records, width), low),
            pltpu.VMEM((records * frames, width), low),
            dma((4, n)),
            dma((4, n)),
            dma((2, n)),
            dma((parts, n)),
            dma((n,)),
            dma((2, n)),
            dma((3, parts)),
            dma((3, parts)),
            dma((n,)),
            dma((records, parts)),
            dma((records, parts)),
            dma((records, records)),
            dma((records, records)),
            dma((2,)),
            dma((2,)),
            dma((8,)),
        ],
        compiler_params=pltpu.CompilerParams(
            collective_id=0, has_side_effects=True, vmem_limit_bytes=60 * 1024 * 1024
        ),
    )(
        length_here,
        flat_input,
        by_record(queries),
        by_record(key_states),
        by_record(value_states),
        flat_grad,
        out_weight[0],
        qkv_weight[0],
        gain,
    )
    return out.reshape(records, frames, width).transpose(1, 0, 2)[None]


def fits(mesh, records, features):
    n = mesh.shape["seq"]
    if n % records or mesh.shape["section"] < 2:
        return False
    parts = n // records
    return features % (parts * 2 * HS) == 0 and n % 2 == 0


def solution(mesh):
    in_specs = (
        P("section", "seq", None, None),
        P("section", None),
        P("section", "seq", None, None),
        P("section", "seq", None, None),
        P("section", "seq", None, None),
        P("section", "seq", None, None),
        P("section", "seq", None),
        P("section", "seq", None),
        P("section", None),
    )
    out_specs = P("section", "seq", None, None)

    def run(*arrays):
        fused = fits(mesh, arrays[2].shape[2], arrays[2].shape[3])
        return jax.shard_map(
            on_device_fused if fused else on_device,
            mesh=mesh,
            in_specs=in_specs,
            out_specs=out_specs,
            check_vma=False,
        )(*arrays)

    return run
```

profile of v0, /device:TPU:27, one launch (start us, length us, event | category | flops | bytes accessed | tf_op | source)
XLA Modules:
  0.0 181.2 jit_solution(15574433382834262160)
XLA Ops:
  0.0 0.0 copy-start
  0.0 0.0 copy-start.1
  0.0 0.7 copy-done
  0.7 0.6 constant_dynamic-slice_fusion
  1.2 0.0 copy-start.2
  1.2 0.0 copy-start.3
  1.2 2.1 %copy.20 = bf16[1,64,4,1024]{3,1,2,0:T(8,128)(2,1)} copy(bf16[1,64,4,1024]{3,2,1,0:T(4,128)(2,1)} %param.11) | data formatting | bytes 1048576 | tf_op args[2]
  3.3 0.0 copy-done.1
  3.3 1.0 copy.13
  4.3 0.0 copy-done.2
  4.3 0.0 copy-done.3
  4.3 1.3 copy_bitcast_fusion.1
  5.6 172.9 %shard_map.91 = bf16[256,1536]{1,0:T(8,128)(2,1)} custom-call(s32[1]{0:T(128)} %bitcast.length_ref, bf16[64,4,1536]{2,1,0:T(4,128)(2,1)} %bitcast.32, bf16[4,64,1024]{2,1,0:T(8,128)(2,1)} %bitcast.30, bf16[4,64,1024]{2,1,0:T(8,128)(2,1)} %get-tuple-element.6.k_ref, bf16[4,64,1024]{2,1,0:T(8,128)(2,1)} %get-tuple-element.5.v_ref, bf16[256,1536]{1,0:T(8,128)(2,1)} %bitcast.28, ...), custom_call_target="tpu_custom_call" | custom-call | tf_op jit(solution)/shard_map/pallas_call | solution.py:609
  178.6 2.6 %copy.19 = bf16[4,64,1536]{2,0,1:T(4,128)(2,1)} copy(bf16[4,64,1536]{2,1,0:T(8,128)(2,1)} %bitcast.29) | data formatting | bytes 1572864 | tf_op jit(solution)/shard_map/reshape | solution.py:657
Async XLA Ops:
  0.0 0.7 copy-start
  0.0 3.3 %copy-start.1 = (bf16[1,64,4,1536]{3,2,1,0:T(4,128)(2,1)S(1)}, bf16[1,64,4,1536]{3,2,1,0:T(4,128)(2,1)}, u32[]{:S(2)}) copy-start(bf16[1,64,4,1536]{3,2,1,0:T(4,128)(2,1)} %param.14) | copy-start | bytes 2359300
  1.2 3.1 %copy-start.2 = (bf16[1,64,4,1024]{3,2,1,0:T(4,128)(2,1)S(1)}, bf16[1,64,4,1024]{3,2,1,0:T(4,128)(2,1)}, u32[]{:S(2)}) copy-start(bf16[1,64,4,1024]{3,2,1,0:T(4,128)(2,1)} %param.13) | copy-start | bytes 1572868
  1.2 3.1 %copy-start.3 = (bf16[1,64,4,1024]{3,2,1,0:T(4,128)(2,1)S(1)}, bf16[1,64,4,1024]{3,2,1,0:T(4,128)(2,1)}, u32[]{:S(2)}) copy-start(bf16[1,64,4,1024]{3,2,1,0:T(4,128)(2,1)} %param.12) | copy-start | bytes 1572868
where the time goes:
time: 181 us
  Pallas kernels  173 us (96%)
  local copies, waits for them, and re-layouts  8.25 us (5%)
    pallas_call x1, Pallas kernels, on_device_fused(): pl.pallas_call(functools.partial(body, (n, sections, records, parts, fram...  173 us

commit v1 on v0

--- a/solution.py
+++ b/solution.py
@@ -182,8 +182,8 @@
     xq,
     xk,
     xv,
-    xg,
-    g_send,
+    xo,
+    g,
     ow,
     w,
     joined,
@@ -193,14 +193,18 @@
     part_recv,
     li_here,
     og_here,
+    lens,
+    gains,
     x_send_sem,
     x_recv_sem,
+    o_send_sem,
+    o_pass_sem,
+    o_recv_sem,
     ow_send_sem,
-    ow_side_sem,
+    ow_pass_sem,
     ow_recv_sem,
     w_send_sem,
-    w_side_sem,
-    w_near_sem,
+    w_pass_sem,
     w_recv_sem,
     side_send_sem,
     side_recv_sem,
@@ -208,16 +212,24 @@
     p_recv_sem,
     s_send_sem,
     s_recv_sem,
-    local_sem,
+    twin_send_sem,
+    twin_recv_sem,
 ):
-    n, sections, groups, parts, frames, cols = dims
+    n, sections, records, parts, frames, cols = dims
     pairs = cols // (2 * HS)
     section = lax.axis_index("section")
     me = lax.axis_index("seq")
-    group = me // parts
+    core = section % 2
+    z = me // parts
     part = me % parts
-    before = (section + sections - 1) % sections
-    after = (section + 1) % sections
+    half = z // 2
+    twin = section + 1 - 2 * core
+    work = section - core + half
+    record = 2 * (z % 2) + core
+    lead = core == half
+    near = z == 1 + half
+    prior = (section + sections - 1) % sections
+    before = (work + sections - 1) % sections
 
     def remote(src, dst, send, recv, sec, dev):
         return pltpu.make_async_remote_copy(
@@ -229,186 +241,267 @@
             device_id_type=pl.DeviceIdType.MESH,
         )
 
+    def either(stays, copy_here, copy_there):
+        @pl.when(stays)
+        def _():
+            copy_here().start()
+
+        @pl.when(jnp.logical_not(stays))
+        def _():
+            copy_there().start()
+
     barrier = pltpu.get_barrier_semaphore()
-
-    def greet(sec, dev):
-        pl.semaphore_signal(
-            barrier, inc=1, device_id=(sec, dev), device_id_type=pl.DeviceIdType.MESH
-        )
-
-    for k in range(1, n):
-        greet(section, (me + k) % n)
-    for k in range(n):
-        greet(before, (me + k) % n)
-        greet(after, (me + k) % n)
-
-    heads = [(q_ref, xq), (k_ref, xk), (v_ref, xv), (g_send, xg)]
-
-    def own(t):
-        src, dst = heads[t]
-        return pltpu.make_async_copy(
-            src.at[group, :, pl.ds(pl.multiple_of(part * cols, cols), cols)],
-            dst.at[me],
-            local_sem.at[t],
-        )
-
-    def exchange(t, k):
-        src, dst = heads[t]
-        to = (me + k) % n
+    for s in range(sections):
+        for k in range(n):
+            if s or k:
+                pl.semaphore_signal(
+                    barrier,
+                    inc=1,
+                    device_id=((section + s) % sections, (me + k) % n),
+                    device_id_type=pl.DeviceIdType.MESH,
+                )
+
+    lane = lax.broadcasted_iota(jnp.int32, lens.shape[1:], 1)
+    lengths = jnp.zeros(lens.shape[1:], jnp.int32)
+    for r in range(records):
+        lengths = jnp.where(lane == r, length_ref[r], lengths)
+    lens[0] = lengths
+
+    pl.semaphore_wait(barrier, sections * n - 1)
+
+    twin_lens = remote(lens.at[0], lens.at[1], twin_send_sem.at[0], twin_recv_sem.at[0], twin, me)
+    twin_gain = remote(gain_ref, gains, twin_send_sem.at[1], twin_recv_sem.at[1], twin, me)
+
+    def seat(r, p):
+        return section - core + r % 2, (2 * core + r // 2) * parts + p
+
+    def turn(i):
+        return (i + 2 * core) % records
+
+    heads = [(q_ref, xq), (k_ref, xk), (v_ref, xv)]
+
+    def x_source(t, r, p):
+        return heads[t][0].at[r, :, pl.ds(p * cols, cols)]
+
+    def x_copy(t, i, p):
+        r = turn(i)
+        sec, dev = seat(r, p)
         return remote(
-            src.at[to // parts, :, pl.ds(pl.multiple_of((to % parts) * cols, cols), cols)],
-            dst.at[me],
-            x_send_sem.at[t, k],
-            x_recv_sem.at[t, k],
+            x_source(t, r, p),
+            heads[t][1].at[me],
+            x_send_sem.at[t, i, p],
+            x_recv_sem.at[t, me],
+            sec,
+            dev,
+        )
+
+    def x_stays(i, p):
+        return lead & (turn(i) == record) & (part == p)
+
+    def x_start(t):
+        for i in range(records):
+            for p in range(parts):
+                either(
+                    x_stays(i, p),
+                    lambda: pltpu.make_async_copy(
+                        x_source(t, turn(i), p), heads[t][1].at[me], x_recv_sem.at[t, me]
+                    ),
+                    lambda: x_copy(t, i, p),
+                )
+
+    def og_source(r):
+        return og_ref.at[pl.ds(pl.multiple_of(r * frames, frames), frames)]
+
+    def o_copy(i):
+        r = turn(i)
+        sec, dev = seat(r, part)
+        return remote(og_source(r), xo.at[me], o_send_sem.at[i], o_recv_sem.at[me], sec, dev)
+
+    def o_stays(i):
+        return lead & (turn(i) == record)
+
+    def o_pass(k):
+        slot = k * parts + part
+        return remote(
+            xo.at[slot],
+            xo.at[slot],
+            o_pass_sem.at[k],
+            o_recv_sem.at[slot],
             section,
-            to,
-        )
-
-    local_ow = pltpu.make_async_copy(ow_in, ow.at[me], local_sem.at[4])
-
-    def piece(t, which):
-        return w_in.at[:, pl.ds(pl.multiple_of((t * parts + which) * cols, cols), cols)]
-
-    def local_w(t):
-        return pltpu.make_async_copy(
-            piece(t, part), w.at[me, :, pl.ds(t * cols, cols)], local_sem.at[5 + t]
-        )
-
-    local_ow.start()
+            z * parts + 1 - part,
+        )
+
+    def lead_z(d):
+        return 1 + core if d == 0 else 3 * core
+
+    ow_slot = me % records
+
+    def ow_copy(d):
+        return remote(
+            ow_in,
+            ow.at[ow_slot],
+            ow_send_sem.at[d],
+            ow_recv_sem.at[ow_slot],
+            section,
+            lead_z(d) * parts + half,
+        )
+
+    def ow_stays(d):
+        return (lead_z(d) == z) & (part == half)
+
+    def w_source(t, p):
+        return w_in.at[:, pl.ds((t * parts + p) * cols, cols)]
+
+    def w_target(t):
+        return w.at[me, :, pl.ds(t * cols, cols)]
+
+    def w_copy(d, p, t):
+        return remote(
+            w_source(t, p),
+            w_target(t),
+            w_send_sem.at[d, p, t],
+            w_recv_sem.at[me],
+            section,
+            lead_z(d) * parts + p,
+        )
+
+    def w_stays(d, p):
+        return (lead_z(d) == z) & (part == p)
+
+    def sends(d):
+        return lead | (d == 0)
+
+    def ow_start(d):
+        either(
+            ow_stays(d),
+            lambda: pltpu.make_async_copy(ow_in, ow.at[ow_slot], ow_recv_sem.at[ow_slot]),
+            lambda: ow_copy(d),
+        )
+
+    def w_start(d):
+        for p in range(parts):
+            for t in range(3):
+                either(
+                    w_stays(d, p),
+                    lambda: pltpu.make_async_copy(w_source(t, p), w_target(t), w_recv_sem.at[me]),
+                    lambda: w_copy(d, p, t),
+                )
+
+    def both_leads(start):
+        start(0)
+
+        @pl.when(lead)
+        def _():
+            start(1)
+
+    def ow_on(slot, way):
+        sec, dev = (twin, me) if way == 0 else (section, 3 * half * parts + part)
+        return remote(
+            ow.at[slot], ow.at[slot], ow_pass_sem.at[way, slot], ow_recv_sem.at[slot], sec, dev
+        )
+
+    def w_on(slot, way):
+        sec, dev = (twin, me) if way == 0 else (section, 3 * half * parts + part)
+        return remote(
+            w.at[slot], w.at[slot], w_pass_sem.at[way, slot], w_recv_sem.at[slot], sec, dev
+        )
+
+    ow_relays = lead & near & (part != half)
+
+    def w_relays(origin):
+        return lead & near & (origin // 2 != half)
+
+    def w_pass(origin):
+        for other in range(parts):
+            slot = origin * parts + other
+            w_on(slot, 0).wait_recv()
+
+            @pl.when(w_relays(origin))
+            def _():
+                w_on(slot, 1).start()
+
+            @pl.when(lead)
+            def _():
+                w_on(slot, 0).start()
+
+    def order(i):
+        return (z, 2 * half + 1 - z % 2, 2 - half, 3 - 3 * half)[i]
+
+    shift_og = remote(og_ref, og_here, s_send_sem.at[0], s_recv_sem.at[0], prior, me)
+    shift_li = remote(li_ref, li_here, s_send_sem.at[1], s_recv_sem.at[1], prior, me)
+
+    twin_lens.start()
+    twin_gain.start()
+    both_leads(ow_start)
+    for i in range(records):
+        r = turn(i)
+        either(
+            o_stays(i),
+            lambda: pltpu.make_async_copy(og_source(r), xo.at[me], o_recv_sem.at[me]),
+            lambda: o_copy(i),
+        )
     for t in range(3):
-        local_w(t).start()
-    for t in range(3):
-        own(t).start()
-    pl.semaphore_wait(barrier, 3 * n - 1)
-    local_ow.wait()
-
-    def ow_hop(slot, way, dev):
-        return remote(
-            ow.at[slot], ow.at[slot], ow_send_sem.at[way, slot], ow_recv_sem.at[slot], section, dev
-        )
-
-    def ow_side(slot, k):
-        return remote(
-            ow.at[slot],
-            ow.at[slot],
-            ow_side_sem.at[k, slot],
-            ow_recv_sem.at[slot],
-            section,
-            group * parts + (part + k) % parts,
-        )
-
-    def w_hop(slot, way, dev):
-        return remote(
-            w.at[slot], w.at[slot], w_send_sem.at[way, slot], w_recv_sem.at[slot], section, dev
-        )
-
-    def w_side(t, k):
-        other = (part + k) % parts
-        return remote(
-            piece(t, other),
-            w.at[me, :, pl.ds(t * cols, cols)],
-            w_side_sem.at[t, k],
-            w_near_sem.at[t, k],
-            section,
-            group * parts + other,
-        )
-
-    def ways(origin, act):
-        @pl.when((origin <= group) & (group + 1 < groups))
-        def _():
-            act(0, me + parts)
-
-        @pl.when((origin >= group) & (group >= 1))
-        def _():
-            act(1, me - parts)
-
-    def ow_pass(origin):
-        slot = origin * parts + part
-        ways(origin, lambda way, dev: ow_hop(slot, way, dev).start())
-        for k in range(1, parts):
-            ow_side(slot, k).start()
-
-    def ow_arrive(origin):
-        @pl.when((origin >= 0) & (origin < groups))
-        def _():
-            slot = origin * parts + part
-            ow_hop(slot, 0, me).wait_recv()
-            ow_pass(origin)
-
-    def w_pass(origin):
-        @pl.when((origin >= 0) & (origin < groups))
-        def _():
-            for other in range(parts):
-                slot = origin * parts + other
-                w_hop(slot, 0, me).wait_recv()
-                ways(origin, lambda way, dev: w_hop(slot, way, dev).start())
-
-    def w_first():
-        for t in range(3):
-            local_w(t).wait()
-        ways(group, lambda way, dev: w_hop(me, way, dev).start())
-        for k in range(1, parts):
-            for t in range(3):
-                w_side(t, k).wait_recv()
-            slot = group * parts + (part + parts - k) % parts
-            ways(group, lambda way, dev: w_hop(slot, way, dev).start())
-
-    ow_pass(group)
-    shift_og = remote(og_ref, og_here, s_send_sem.at[0], s_recv_sem.at[0], before, me)
-    shift_li = remote(li_ref, li_here, s_send_sem.at[1], s_recv_sem.at[1], before, me)
-    for k in range(1, n):
-        exchange(0, k).start()
+        x_start(t)
     shift_og.start()
     shift_li.start()
-    for s in range(1, groups):
-        ow_arrive(group - s)
-        ow_arrive(group + s)
-    for k in range(1, parts):
-        for t in range(3):
-            w_side(t, k).start()
-    for t in (1, 2):
-        for k in range(1, n):
-            exchange(t, k).start()
-    w_first()
-    for origin in range(groups):
-        for k in range(1, parts):
-            ow_side(origin * parts + (part + k) % parts, k).wait_recv()
-
-    features = groups * parts
+
+    for slot in range(records):
+        ow_on(slot, 0).wait_recv()
+
+        @pl.when(ow_relays)
+        def _():
+            ow_on(slot, 1).start()
+
+        @pl.when(lead)
+        def _():
+            ow_on(slot, 0).start()
+
+    for k in range(records):
+        o_pass(k).wait_recv()
+        o_pass(k).start()
+    both_leads(w_start)
+    for k in range(records):
+        slot = k * parts + 1 - part
+        remote(
+            xo.at[slot], xo.at[slot], o_pass_sem.at[k], o_recv_sem.at[slot], section, me
+        ).wait_recv()
+
+    length = n * frames
     rows_here = ow.shape[1]
 
     def project(i, carry):
         weight = ow[pl.ds(2 * i, 2)].reshape(2 * rows_here, ow.shape[2])
-        result = lax.dot_general(
-            og_ref[...], weight, ROW_DOT, preferred_element_type=jnp.float32
+        grads = xo[...].reshape(length, xo.shape[2])
+        lanes = pl.ds(pl.multiple_of(i * 2 * rows_here, 2 * rows_here), 2 * rows_here)
+        g[:, lanes] = lax.dot_general(
+            grads, weight, ROW_DOT, preferred_element_type=jnp.float32
         ).astype(jnp.bfloat16)
-        g_send[:, :, pl.ds(pl.multiple_of(i * 2 * rows_here, 2 * rows_here), 2 * rows_here)] = (
-            result.reshape(groups, frames, 2 * rows_here)
-        )
         return carry
 
-    lax.fori_loop(0, features // 2, project, 0)
-    own(3).start()
-    for k in range(1, n):
-        exchange(3, k).start()
-    w_pass(group - 1)
-    w_pass(group + 1)
-    for t in range(4):
-        own(t).wait()
-        for k in range(1, n):
-            exchange(t, k).wait_recv()
-
-    length = n * frames
-    valid = length_ref[0]
+    lax.fori_loop(0, cols // (2 * rows_here), project, 0)
+    twin_lens.wait_recv()
+    twin_gain.wait_recv()
+    for t in range(3):
+        for j in range(n):
+            remote(
+                heads[t][1].at[j],
+                heads[t][1].at[j],
+                x_send_sem.at[t, 0, 0],
+                x_recv_sem.at[t, j],
+                section,
+                me,
+            ).wait_recv()
+
+    valid = jnp.where(lead, lens[0], lens[1])
+    valid = jnp.sum(jnp.where(lane == record, valid, 0), axis=1, keepdims=True)[:1]
     keys_ok = lax.broadcasted_iota(jnp.int32, (length, 1), 0) < valid
     low_lanes = lax.broadcasted_iota(jnp.int32, (length, 2 * HS), 1) < HS
     scale = HS ** (-0.5)
 
     def attend(j, carry):
         lanes = pl.ds(pl.multiple_of(j * 2 * HS, 2 * HS), 2 * HS)
-        queries, keys, values, grads = (
-            x[:, :, lanes].reshape(length, 2 * HS) for x in (xq, xk, xv, xg)
-        )
+        queries, keys, values = (x[:, :, lanes].reshape(length, 2 * HS) for x in (xq, xk, xv))
+        grads = g[:, lanes]
         keys_across = keys.T
         nothing = jnp.zeros_like(keys)
         halves = []
@@ -444,84 +537,98 @@
             at = pl.multiple_of(t * cols + j * 2 * HS, 2 * HS)
             joined[:, pl.ds(at, 2 * HS)] = both.astype(jnp.bfloat16)
 
-        @pl.when(j == pairs - 2)
-        def _():
-            w_pass(group - 2)
-            w_pass(group + 2)
+        for i in range(records - 1):
+
+            @pl.when(j == max(pairs - (records - 1) + i, 0))
+            def _():
+                w_pass(order(i))
 
         return carry
 
-    if pairs < 2:
-        w_pass(group - 2)
-        w_pass(group + 2)
     lax.fori_loop(0, pairs, attend, 0)
 
-    def side_copy(origin, k):
-        other = (part + k) % parts
+    def side_copy(origin):
+        other = 1 - part
         return remote(
             part_send.at[origin, other],
-            side_recv.at[origin, k],
-            side_send_sem.at[origin, k],
-            side_recv_sem.at[origin, k],
+            side_recv.at[origin],
+            side_send_sem.at[origin],
+            side_recv_sem.at[origin],
             section,
-            group * parts + other,
+            z * parts + other,
         )
 
     def sum_copy(origin, to):
         return remote(
             sum_send.at[origin, to],
-            part_recv.at[group, origin],
+            part_recv.at[record, origin],
             p_send_sem.at[origin, to],
-            p_recv_sem.at[group, origin],
+            p_recv_sem.at[record, origin],
             before,
             to * parts + part,
         )
 
-    blocks = 2 * groups - 1
-
-    def origin_of(i):
-        return group + ((i + 1) // 2) * (1 - 2 * (i % 2))
-
-    def norm_block(i, carry):
-        earlier = origin_of(i - 2)
-
-        @pl.when((i >= 2) & (earlier >= 0) & (earlier < groups))
-        def _():
-            total = part_send[earlier, part].astype(jnp.float32)
-            for k in range(1, parts):
-                side_copy(earlier, k).wait_recv()
-                total = total + side_recv[earlier, k].astype(jnp.float32)
-            sum_send[earlier] = total.astype(jnp.bfloat16)
-            for k in range(groups):
-                sum_copy(earlier, (group + k) % groups).start()
-
-        origin = origin_of(i)
-
-        @pl.when((i >= 5) & (i < blocks))
-        def _():
+    def sum_stays(to):
+        return (before == section) & (to == z)
+
+    def norm_block(origin):
+        weight = w[pl.ds(origin * parts, parts)].reshape(parts * w.shape[1], w.shape[2])
+        sums = lax.dot_general(
+            joined[...], weight, ROW_DOT, preferred_element_type=jnp.float32
+        )
+        gain = jnp.where(lead, gain_ref[origin], gains[origin])
+        sums = (sums * gain).astype(jnp.bfloat16)
+        sums = sums.reshape(records, parts, frames, sums.shape[1])
+        for other in range(parts):
+            part_send[origin, other] = sums[:, other]
+        side_copy(origin).start()
+
+    def norm_send(origin):
+        side_copy(origin).wait_recv()
+        total = part_send[origin, part].astype(jnp.float32)
+        total = total + side_recv[origin].astype(jnp.float32)
+        sum_send[origin] = total.astype(jnp.bfloat16)
+        for k in range(records):
+            to = (z + k) % records
+            either(
+                sum_stays(to),
+                lambda: pltpu.make_async_copy(
+                    sum_send.at[origin, to],
+                    part_recv.at[record, origin],
+                    p_recv_sem.at[record, origin],
+                ),
+                lambda: sum_copy(origin, to),
+            )
+
+    def norm(i, carry):
+        origin = jnp.where(
+            i == 0, order(0), jnp.where(i == 1, order(1), jnp.where(i == 2, order(2), order(3)))
+        )
+        last = jnp.where(i == 1, order(0), jnp.where(i == 2, order(1), order(2)))
+
+        @pl.when(i == records - 1)
+        def _():
+            norm_send(last)
             w_pass(origin)
 
-        @pl.when((i < blocks) & (origin >= 0) & (origin < groups))
-        def _():
-            weight = w[pl.ds(origin * parts, parts)].reshape(parts * w.shape[1], w.shape[2])
-            sums = lax.dot_general(
-                joined[...], weight, ROW_DOT, preferred_element_type=jnp.float32
-            )
-            sums = (sums * gain_ref[origin]).astype(jnp.bfloat16)
-            sums = sums.reshape(groups, parts, frames, sums.shape[1])
-            for other in range(parts):
-                part_send[origin, other] = sums[:, other]
-            for k in range(1, parts):
-                side_copy(origin, k).start()
+        norm_block(origin)
+
+        @pl.when((i > 0) & (i < records - 1))
+        def _():
+            norm_send(last)
+
+        @pl.when(i == records - 1)
+        def _():
+            norm_send(origin)
 
         return carry
 
-    lax.fori_loop(0, blocks + 2, norm_block, 0)
+    lax.fori_loop(0, records, norm, 0)
 
     shift_og.wait_recv()
     shift_li.wait_recv()
-    for src in range(groups):
-        for origin in range(groups):
+    for src in range(records):
+        for origin in range(records):
             remote(
                 sum_send.at[origin, 0],
                 part_recv.at[src, origin],
@@ -541,7 +648,7 @@
         deviation = 1.0 / jnp.sqrt(var + EPSILON)
         normal = centered * deviation
         scaled = []
-        for origin in range(groups):
+        for origin in range(records):
             scaled.append(part_recv[r, origin].astype(jnp.float32))
         scaled = jnp.concatenate(scaled, axis=1)
         average = jnp.sum(scaled, axis=1, keepdims=True) * (1.0 / width)
@@ -549,29 +656,55 @@
         branch = deviation * (scaled - average - normal * along)
         out_ref[rows, :] = (og_here[rows, :].astype(jnp.float32) + branch).astype(jnp.bfloat16)
 
-    for r in range(groups):
+    for r in range(records):
         finish(r)
 
-    for t in range(4):
-        for k in range(1, n):
-            exchange(t, k).wait_send()
-    for origin in range(groups):
-        slot = origin * parts + part
-        ways(origin, lambda way, dev: ow_hop(slot, way, dev).wait_send())
-        for k in range(1, parts):
-            ow_side(slot, k).wait_send()
-        for other in range(parts):
-            w_slot = origin * parts + other
-            ways(origin, lambda way, dev: w_hop(w_slot, way, dev).wait_send())
-        for to in range(groups):
-            sum_copy(origin, to).wait_send()
-        for k in range(1, parts):
-            side_copy(origin, k).wait_send()
-    for k in range(1, parts):
-        for t in range(3):
-            w_side(t, k).wait_send()
+    def sent(stays, copy):
+        @pl.when(jnp.logical_not(stays))
+        def _():
+            copy.wait_send()
+
+    twin_lens.wait_send()
+    twin_gain.wait_send()
     shift_og.wait_send()
     shift_li.wait_send()
+    for i in range(records):
+        sent(o_stays(i), o_copy(i))
+        o_pass(i).wait_send()
+        for t in range(3):
+            for p in range(parts):
+                sent(x_stays(i, p), x_copy(t, i, p))
+    for d in range(2):
+
+        @pl.when(sends(d))
+        def _():
+            sent(ow_stays(d), ow_copy(d))
+            for p in range(parts):
+                for t in range(3):
+                    sent(w_stays(d, p), w_copy(d, p, t))
+
+    @pl.when(ow_relays)
+    def _():
+        for slot in range(records):
+            ow_on(slot, 1).wait_send()
+
+    @pl.when(lead)
+    def _():
+        for slot in range(records):
+            ow_on(slot, 0).wait_send()
+        for slot in range(n):
+            w_on(slot, 0).wait_send()
+
+    for origin in range(records):
+
+        @pl.when(w_relays(origin))
+        def _():
+            for other in range(parts):
+                w_on(origin * parts + other, 1).wait_send()
+
+        side_copy(origin).wait_send()
+        for to in range(records):
+            sent(sum_stays(to), sum_copy(origin, to))
 
 
 def on_device_fused(
@@ -594,13 +727,10 @@
     ow_rows = out_weight.shape[1]
     w_rows = qkv_weight.shape[1]
     block = parts * w_rows
-    group = lax.axis_index("seq") // parts
-    length_here = lax.dynamic_slice(lengths[0], (group,), (1,))
 
     def by_record(x):
         return x[0].transpose(1, 0, 2)
 
-    flat_input = layer_input[0]
     flat_grad = by_record(out_grad).reshape(records * frames, width)
     gain = norm_gain[0].reshape(records, 1, block)
     vmem = pl.BlockSpec(memory_space=pltpu.VMEM)
@@ -611,41 +741,47 @@
         out_shape=jax.ShapeDtypeStruct((records * frames, width), low),
         in_specs=[pl.BlockSpec(memory_space=pltpu.SMEM)] + [vmem] * 8,
         out_specs=vmem,
-        scratch_shapes=[pltpu.VMEM((n, frames, cols), low)] * 4
+        scratch_shapes=[pltpu.VMEM((n, frames, cols), low)] * 3
         + [
-            pltpu.VMEM((records, frames, features), low),
-            pltpu.VMEM((n, ow_rows, width), low),
+            pltpu.VMEM((n, frames, width), low),
+            pltpu.VMEM((n * frames, cols), low),
+            pltpu.VMEM((records, ow_rows, width), low),
             pltpu.VMEM((n, w_rows, 3 * cols), low),
             pltpu.VMEM((n * frames, 3 * cols), low),
             pltpu.VMEM((records, parts, records, frames, block), low),
-            pltpu.VMEM((records, parts, records, frames, block), low),
+            pltpu.VMEM((records, records, frames, block), low),
             pltpu.VMEM((records, records, frames, block), low),
             pltpu.VMEM((records, records, frames, block), low),
             pltpu.VMEM((frames, records, width), low),
             pltpu.VMEM((records * frames, width), low),
-            dma((4, n)),
-            dma((4, n)),
+            pltpu.VMEM((2, 8, 128), jnp.int32),
+            pltpu.VMEM((records, 1, block), jnp.float32),
+            dma((3, records, parts)),
+            dma((3, n)),
+            dma((records,)),
+            dma((records,)),
+            dma((n,)),
+            dma((2,)),
+            dma((2, records)),
+            dma((records,)),
+            dma((2, parts, 3)),
             dma((2, n)),
-            dma((parts, n)),
             dma((n,)),
-            dma((2, n)),
-            dma((3, parts)),
-            dma((3, parts)),
-            dma((n,)),
-            dma((records, parts)),
-            dma((records, parts)),
+            dma((records,)),
+            dma((records,)),
             dma((records, records)),
             dma((records, records)),
             dma((2,)),
             dma((2,)),
-            dma((8,)),
+            dma((2,)),
+            dma((2,)),
         ],
         compiler_params=pltpu.CompilerParams(
             collective_id=0, has_side_effects=True, vmem_limit_bytes=60 * 1024 * 1024
         ),
     )(
-        length_here,
-        flat_input,
+        lengths[0],
+        layer_input[0],
         by_record(queries),
         by_record(key_states),
         by_record(value_states),
@@ -659,10 +795,9 @@
 
 def fits(mesh, records, features):
     n = mesh.shape["seq"]
-    if n % records or mesh.shape["section"] < 2:
+    if n != 2 * records or records != 4 or mesh.shape["section"] % 2:
         return False
-    parts = n // records
-    return features % (parts * 2 * HS) == 0 and n % 2 == 0
+    return features % (n * HS) == 0
 
 
 def solution(mesh):

time: 181 us -> 160 us (0.88)
  Pallas kernels: 173 us -> 153 us
    pallas_call x1, Pallas kernels: 173 us -> 153 us  [on_device_fused(): pl.pallas_call(functools.partial(body, (n, sections, records, parts, fram...]
where the time goes in v1:
time: 160 us
  Pallas kernels  153 us (96%)
  local copies, waits for them, and re-layouts  7.07 us (4%)
    pallas_call x1, Pallas kernels, on_device_fused(): pl.pallas_call(functools.partial(body, (n, sections, records, parts, fram...  153 us

profile of v1, /device:TPU:27, one launch (start us, length us, event | category | flops | bytes accessed | tf_op | source)
XLA Modules:
  0.0 159.9 jit_solution(9869145934642615755)
XLA Ops:
  0.0 0.0 copy-start
  0.0 0.0 copy-start.1
  0.0 0.0 copy-start.2
  0.0 2.1 %copy.20 = bf16[1,64,4,1024]{3,1,2,0:T(8,128)(2,1)} copy(bf16[1,64,4,1024]{3,2,1,0:T(4,128)(2,1)} %param.11) | data formatting | bytes 1048576 | tf_op args[2]
  2.1 0.0 copy-done
  2.1 1.0 copy.13
  3.2 0.0 copy-done.1
  3.2 0.0 copy-done.2
  3.2 1.3 copy_bitcast_fusion.1
  4.5 152.8 %shard_map.91 = bf16[256,1536]{1,0:T(8,128)(2,1)} custom-call(s32[4]{0:T(128)} %bitcast.36, bf16[64,4,1536]{2,1,0:T(4,128)(2,1)} %bitcast.32, bf16[4,64,1024]{2,1,0:T(8,128)(2,1)} %bitcast.30, bf16[4,64,1024]{2,1,0:T(8,128)(2,1)} %get-tuple-element.6.k_ref, bf16[4,64,1024]{2,1,0:T(8,128)(2,1)} %get-tuple-element.5.v_ref, bf16[256,1536]{1,0:T(8,128)(2,1)} %bitcast.28, ...), custom_call_target="tpu_custom_call" | custom-call | tf_op jit(solution)/shard_map/pallas_call | solution.py:739
  157.2 2.6 %copy.19 = bf16[4,64,1536]{2,0,1:T(4,128)(2,1)} copy(bf16[4,64,1536]{2,1,0:T(8,128)(2,1)} %bitcast.29) | data formatting | bytes 1572864 | tf_op jit(solution)/shard_map/reshape | solution.py:793
Async XLA Ops:
  0.0 2.1 %copy-start = (bf16[1,64,4,1536]{3,2,1,0:T(4,128)(2,1)S(1)}, bf16[1,64,4,1536]{3,2,1,0:T(4,128)(2,1)}, u32[]{:S(2)}) copy-start(bf16[1,64,4,1536]{3,2,1,0:T(4,128)(2,1)} %param.14) | copy-start | bytes 2359300
  0.0 3.2 %copy-start.1 = (bf16[1,64,4,1024]{3,2,1,0:T(4,128)(2,1)S(1)}, bf16[1,64,4,1024]{3,2,1,0:T(4,128)(2,1)}, u32[]{:S(2)}) copy-start(bf16[1,64,4,1024]{3,2,1,0:T(4,128)(2,1)} %param.13) | copy-start | bytes 1572868
  0.0 3.2 %copy-start.2 = (bf16[1,64,4,1024]{3,2,1,0:T(4,128)(2,1)S(1)}, bf16[1,64,4,1024]{3,2,1,0:T(4,128)(2,1)}, u32[]{:S(2)}) copy-start(bf16[1,64,4,1024]{3,2,1,0:T(4,128)(2,1)} %param.12) | copy-start | bytes 1572868

commit v2 on v1

--- a/solution.py
+++ b/solution.py
@@ -185,6 +185,7 @@
     xo,
     g,
     ow,
+    ow_via,
     w,
     joined,
     part_send,
@@ -203,6 +204,8 @@
     ow_send_sem,
     ow_pass_sem,
     ow_recv_sem,
+    via_send_sem,
+    via_recv_sem,
     w_send_sem,
     w_pass_sem,
     w_recv_sem,
@@ -346,11 +349,45 @@
             lead_z(d) * parts + half,
         )
 
+    through = part != half
+
+    def via_copy():
+        return remote(
+            ow_in,
+            ow_via.at[z % 2],
+            via_send_sem.at[0, 0],
+            via_recv_sem.at[z % 2],
+            section,
+            (1 + core) * parts + part,
+        )
+
+    def via_on(k, way):
+        slot = k * parts + part
+        dev = (1 + half if way == 0 else 3 * half) * parts + 1 - half
+        return remote(
+            ow_via.at[k],
+            ow.at[slot],
+            via_send_sem.at[1 + way, k],
+            ow_recv_sem.at[slot],
+            section,
+            dev,
+        )
+
+    def near_copy():
+        return remote(
+            ow_in,
+            ow.at[ow_slot],
+            ow_send_sem.at[0],
+            ow_recv_sem.at[ow_slot],
+            section,
+            (1 + core) * parts + part,
+        )
+
     def ow_stays(d):
         return (lead_z(d) == z) & (part == half)
 
     def w_source(t, p):
-        return w_in.at[:, pl.ds((t * parts + p) * cols, cols)]
+        return w_in.at[:, pl.ds(pl.multiple_of((t * parts + p) * cols, cols), cols)]
 
     def w_target(t):
         return w.at[me, :, pl.ds(t * cols, cols)]
@@ -360,7 +397,7 @@
             w_source(t, p),
             w_target(t),
             w_send_sem.at[d, p, t],
-            w_recv_sem.at[me],
+            w_recv_sem.at[me, t],
             section,
             lead_z(d) * parts + p,
         )
@@ -378,21 +415,21 @@
             lambda: ow_copy(d),
         )
 
-    def w_start(d):
-        for p in range(parts):
-            for t in range(3):
-                either(
-                    w_stays(d, p),
-                    lambda: pltpu.make_async_copy(w_source(t, p), w_target(t), w_recv_sem.at[me]),
-                    lambda: w_copy(d, p, t),
-                )
-
-    def both_leads(start):
-        start(0)
-
-        @pl.when(lead)
-        def _():
-            start(1)
+    def w_start(t, d, p):
+        either(
+            w_stays(d, p),
+            lambda: pltpu.make_async_copy(w_source(t, p), w_target(t), w_recv_sem.at[me, t]),
+            lambda: w_copy(d, p, t),
+        )
+
+    def w_starts(t):
+        for q in range(parts):
+            p = (part + q) % parts
+            w_start(t, 0, p)
+
+            @pl.when(lead)
+            def _():
+                w_start(t, 1, p)
 
     def ow_on(slot, way):
         sec, dev = (twin, me) if way == 0 else (section, 3 * half * parts + part)
@@ -400,29 +437,30 @@
             ow.at[slot], ow.at[slot], ow_pass_sem.at[way, slot], ow_recv_sem.at[slot], sec, dev
         )
 
-    def w_on(slot, way):
+    def w_on(slot, t, way):
         sec, dev = (twin, me) if way == 0 else (section, 3 * half * parts + part)
-        return remote(
-            w.at[slot], w.at[slot], w_pass_sem.at[way, slot], w_recv_sem.at[slot], sec, dev
-        )
-
-    ow_relays = lead & near & (part != half)
+        at = w.at[slot, :, pl.ds(t * cols, cols)]
+        return remote(at, at, w_pass_sem.at[way, slot, t], w_recv_sem.at[slot, t], sec, dev)
+
+    relays = lead & near
+    ow_relays = relays & (part != half)
+    via_relays = relays & (part == half)
 
     def w_relays(origin):
         return lead & near & (origin // 2 != half)
 
-    def w_pass(origin):
-        for other in range(parts):
-            slot = origin * parts + other
-            w_on(slot, 0).wait_recv()
+    def w_pass(origin, t):
+        for q in range(parts):
+            slot = origin * parts + (part + q) % parts
+            w_on(slot, t, 0).wait_recv()
 
             @pl.when(w_relays(origin))
             def _():
-                w_on(slot, 1).start()
+                w_on(slot, t, 1).start()
 
             @pl.when(lead)
             def _():
-                w_on(slot, 0).start()
+                w_on(slot, t, 0).start()
 
     def order(i):
         return (z, 2 * half + 1 - z % 2, 2 - half, 3 - 3 * half)[i]
@@ -432,7 +470,21 @@
 
     twin_lens.start()
     twin_gain.start()
-    both_leads(ow_start)
+    @pl.when(lead)
+    def _():
+        ow_start(0)
+        ow_start(1)
+
+    @pl.when(jnp.logical_not(lead))
+    def _():
+        @pl.when(part == half)
+        def _():
+            near_copy().start()
+
+        @pl.when(part != half)
+        def _():
+            via_copy().start()
+
     for i in range(records):
         r = turn(i)
         either(
@@ -442,15 +494,37 @@
         )
     for t in range(3):
         x_start(t)
+    for t in range(3):
+        w_starts(t)
     shift_og.start()
     shift_li.start()
 
+    @pl.when(via_relays)
+    def _():
+        for k in range(2):
+            remote(
+                ow_via.at[k],
+                ow_via.at[k],
+                via_send_sem.at[0, k],
+                via_recv_sem.at[k],
+                section,
+                me,
+            ).wait_recv()
+            via_on(k, 1).start()
+            via_on(k, 0).start()
+
     for slot in range(records):
         ow_on(slot, 0).wait_recv()
-
-        @pl.when(ow_relays)
-        def _():
-            ow_on(slot, 1).start()
+        if slot % parts == 0:
+
+            @pl.when(ow_relays & (part == 0))
+            def _():
+                ow_on(slot, 1).start()
+        else:
+
+            @pl.when(ow_relays & (part == 1))
+            def _():
+                ow_on(slot, 1).start()
 
         @pl.when(lead)
         def _():
@@ -459,7 +533,6 @@
     for k in range(records):
         o_pass(k).wait_recv()
         o_pass(k).start()
-    both_leads(w_start)
     for k in range(records):
         slot = k * parts + 1 - part
         remote(
@@ -497,6 +570,19 @@
     keys_ok = lax.broadcasted_iota(jnp.int32, (length, 1), 0) < valid
     low_lanes = lax.broadcasted_iota(jnp.int32, (length, 2 * HS), 1) < HS
     scale = HS ** (-0.5)
+
+    plan = [(0, 0, 0), (0, 0, 1), (0, 0, 2), (1, 1, 0), (1, 1, 1), (1, 1, 2)]
+    plan += [(3, 2, 0), (3, 3, 0), (6, 2, 1), (6, 3, 1)]
+    steps = 2 * pairs
+
+    def between(step):
+        for at in sorted({s for s, _, _ in plan}):
+
+            @pl.when(step == min(at, steps - 1))
+            def _():
+                for s, i, t in plan:
+                    if s == at:
+                        w_pass(order(i), t)
 
     def attend(j, carry):
         lanes = pl.ds(pl.multiple_of(j * 2 * HS, 2 * HS), 2 * HS)
@@ -529,6 +615,7 @@
                 keys_across[h * HS : (h + 1) * HS], grad_scores, preferred_element_type=jnp.float32
             )
             halves.append((query_grad, key_grad, value_grad))
+            between(2 * j + h)
         (query_0, key_0, value_0), (query_1, key_1, value_1) = halves
         query_both = (jnp.concatenate([query_0, query_1], axis=0) * scale).T
         key_both = jnp.where(low_lanes, key_0, key_1) * scale
@@ -536,12 +623,6 @@
         for t, both in enumerate((query_both, key_both, value_both)):
             at = pl.multiple_of(t * cols + j * 2 * HS, 2 * HS)
             joined[:, pl.ds(at, 2 * HS)] = both.astype(jnp.bfloat16)
-
-        for i in range(records - 1):
-
-            @pl.when(j == max(pairs - (records - 1) + i, 0))
-            def _():
-                w_pass(order(i))
 
         return carry
 
@@ -606,14 +687,15 @@
         )
         last = jnp.where(i == 1, order(0), jnp.where(i == 2, order(1), order(2)))
 
-        @pl.when(i == records - 1)
+        @pl.when(i == 2)
         def _():
             norm_send(last)
-            w_pass(origin)
+            w_pass(order(2), 2)
+            w_pass(order(3), 2)
 
         norm_block(origin)
 
-        @pl.when((i > 0) & (i < records - 1))
+        @pl.when((i == 1) | (i == records - 1))
         def _():
             norm_send(last)
 
@@ -678,14 +760,32 @@
 
         @pl.when(sends(d))
         def _():
-            sent(ow_stays(d), ow_copy(d))
             for p in range(parts):
                 for t in range(3):
                     sent(w_stays(d, p), w_copy(d, p, t))
 
-    @pl.when(ow_relays)
+        @pl.when(lead)
+        def _():
+            sent(ow_stays(d), ow_copy(d))
+
+    @pl.when(jnp.logical_not(lead) & (part == half))
     def _():
-        for slot in range(records):
+        near_copy().wait_send()
+
+    @pl.when(jnp.logical_not(lead) & (part != half))
+    def _():
+        via_copy().wait_send()
+
+    @pl.when(via_relays)
+    def _():
+        for k in range(2):
+            via_on(k, 1).wait_send()
+            via_on(k, 0).wait_send()
+
+    for slot in range(records):
+
+        @pl.when(ow_relays & (part == slot % parts))
+        def _():
             ow_on(slot, 1).wait_send()
 
     @pl.when(lead)
@@ -693,14 +793,16 @@
         for slot in range(records):
             ow_on(slot, 0).wait_send()
         for slot in range(n):
-            w_on(slot, 0).wait_send()
+            for t in range(3):
+                w_on(slot, t, 0).wait_send()
 
     for origin in range(records):
 
         @pl.when(w_relays(origin))
         def _():
             for other in range(parts):
-                w_on(origin * parts + other, 1).wait_send()
+                for t in range(3):
+                    w_on(origin * parts + other, t, 1).wait_send()
 
         side_copy(origin).wait_send()
         for to in range(records):
@@ -746,6 +848,7 @@
             pltpu.VMEM((n, frames, width), low),
             pltpu.VMEM((n * frames, cols), low),
             pltpu.VMEM((records, ow_rows, width), low),
+            pltpu.VMEM((2, ow_rows, width), low),
             pltpu.VMEM((n, w_rows, 3 * cols), low),
             pltpu.VMEM((n * frames, 3 * cols), low),
             pltpu.VMEM((records, parts, records, frames, block), low),
@@ -764,9 +867,11 @@
             dma((2,)),
             dma((2, records)),
             dma((records,)),
+            dma((3, 2)),
+            dma((2,)),
             dma((2, parts, 3)),
-            dma((2, n)),
-            dma((n,)),
+            dma((2, n, 3)),
+            dma((n, 3)),
             dma((records,)),
             dma((records,)),
             dma((records, records)),

time: 160 us -> 150 us (0.938)
  Pallas kernels: 153 us -> 142 us
    pallas_call x1, Pallas kernels: 153 us -> 142 us  [on_device_fused(): pl.pallas_call(functools.partial(body, (n, sections, records, parts, fram...]
where the time goes in v2:
time: 150 us; the launch traced here: 149 us
  Pallas kernels  142 us (95%)
  local copies, waits for them, and re-layouts  7.07 us (5%)
    pallas_call x1, Pallas kernels, on_device_fused(): pl.pallas_call(functools.partial(body, (n, sections, records, parts, fram...  142 us

profile of v2, /device:TPU:27, one launch (start us, length us, event | category | flops | bytes accessed | tf_op | source)
XLA Modules:
  0.0 149.5 jit_solution(12328322451887433781)
XLA Ops:
  0.0 0.0 copy-start
  0.0 0.0 copy-start.1
  0.0 0.0 copy-start.2
  0.0 2.1 %copy.20 = bf16[1,64,4,1024]{3,1,2,0:T(8,128)(2,1)} copy(bf16[1,64,4,1024]{3,2,1,0:T(4,128)(2,1)} %param.11) | data formatting | bytes 1048576 | tf_op args[2]
  2.1 0.0 copy-done
  2.1 1.0 copy.13
  3.2 0.0 copy-done.1
  3.2 0.0 copy-done.2
  3.2 1.3 copy_bitcast_fusion.1
  4.5 142.4 %shard_map.91 = bf16[256,1536]{1,0:T(8,128)(2,1)} custom-call(s32[4]{0:T(128)} %bitcast.36, bf16[64,4,1536]{2,1,0:T(4,128)(2,1)} %bitcast.32, bf16[4,64,1024]{2,1,0:T(8,128)(2,1)} %bitcast.30, bf16[4,64,1024]{2,1,0:T(8,128)(2,1)} %get-tuple-element.6.k_ref, bf16[4,64,1024]{2,1,0:T(8,128)(2,1)} %get-tuple-element.5.v_ref, bf16[256,1536]{1,0:T(8,128)(2,1)} %bitcast.28, ...), custom_call_target="tpu_custom_call" | custom-call | tf_op jit(solution)/shard_map/pallas_call | solution.py:841
  146.9 2.6 %copy.19 = bf16[4,64,1536]{2,0,1:T(4,128)(2,1)} copy(bf16[4,64,1536]{2,1,0:T(8,128)(2,1)} %bitcast.29) | data formatting | bytes 1572864 | tf_op jit(solution)/shard_map/reshape | solution.py:898
Async XLA Ops:
  0.0 2.1 %copy-start = (bf16[1,64,4,1536]{3,2,1,0:T(4,128)(2,1)S(1)}, bf16[1,64,4,1536]{3,2,1,0:T(4,128)(2,1)}, u32[]{:S(2)}) copy-start(bf16[1,64,4,1536]{3,2,1,0:T(4,128)(2,1)} %param.14) | copy-start | bytes 2359300
  0.0 3.2 %copy-start.1 = (bf16[1,64,4,1024]{3,2,1,0:T(4,128)(2,1)S(1)}, bf16[1,64,4,1024]{3,2,1,0:T(4,128)(2,1)}, u32[]{:S(2)}) copy-start(bf16[1,64,4,1024]{3,2,1,0:T(4,128)(2,1)} %param.13) | copy-start | bytes 1572868
  0.0 3.2 %copy-start.2 = (bf16[1,64,4,1024]{3,2,1,0:T(4,128)(2,1)S(1)}, bf16[1,64,4,1024]{3,2,1,0:T(4,128)(2,1)}, u32[]{:S(2)}) copy-start(bf16[1,64,4,1024]{3,2,1,0:T(4,128)(2,1)} %param.12) | copy-start | bytes 1572868

commit v3 on v2

--- a/solution.py
+++ b/solution.py
@@ -171,14 +171,18 @@
     dims,
     length_ref,
     li_ref,
+    q_in,
+    k_in,
+    v_in,
+    og_in,
+    ow_in,
+    w_in,
+    gain_ref,
+    out_ref,
     q_ref,
     k_ref,
     v_ref,
     og_ref,
-    ow_in,
-    w_in,
-    gain_ref,
-    out_ref,
     xq,
     xk,
     xv,
@@ -194,6 +198,8 @@
     part_recv,
     li_here,
     og_here,
+    normals,
+    deviations,
     lens,
     gains,
     x_send_sem,
@@ -270,6 +276,14 @@
         lengths = jnp.where(lane == r, length_ref[r], lengths)
     lens[0] = lengths
 
+    def by_record(source, target):
+        for r in range(records):
+            if len(target.shape) == 2:
+                target[r * frames : (r + 1) * frames] = source[:, r, :]
+            else:
+                target[r] = source[:, r, :]
+
+    by_record(og_in, og_ref)
     pl.semaphore_wait(barrier, sections * n - 1)
 
     twin_lens = remote(lens.at[0], lens.at[1], twin_send_sem.at[0], twin_recv_sem.at[0], twin, me)
@@ -422,14 +436,10 @@
             lambda: w_copy(d, p, t),
         )
 
-    def w_starts(t):
+    def w_starts(t, d):
         for q in range(parts):
             p = (part + q) % parts
-            w_start(t, 0, p)
-
-            @pl.when(lead)
-            def _():
-                w_start(t, 1, p)
+            w_start(t, d, p)
 
     def ow_on(slot, way):
         sec, dev = (twin, me) if way == 0 else (section, 3 * half * parts + part)
@@ -492,10 +502,14 @@
             lambda: pltpu.make_async_copy(og_source(r), xo.at[me], o_recv_sem.at[me]),
             lambda: o_copy(i),
         )
+    by_record(q_in, q_ref)
+    x_start(0)
+    by_record(k_in, k_ref)
+    x_start(1)
+    by_record(v_in, v_ref)
+    x_start(2)
     for t in range(3):
-        x_start(t)
-    for t in range(3):
-        w_starts(t)
+        w_starts(t, 0)
     shift_og.start()
     shift_li.start()
 
@@ -513,26 +527,33 @@
             via_on(k, 1).start()
             via_on(k, 0).start()
 
-    for slot in range(records):
-        ow_on(slot, 0).wait_recv()
-        if slot % parts == 0:
-
-            @pl.when(ow_relays & (part == 0))
-            def _():
-                ow_on(slot, 1).start()
-        else:
-
-            @pl.when(ow_relays & (part == 1))
-            def _():
-                ow_on(slot, 1).start()
-
-        @pl.when(lead)
-        def _():
+    @pl.when(ow_relays)
+    def _():
+        for k in range(2):
+            slot = k * parts + part
+            ow_on(slot, 0).wait_recv()
+            ow_on(slot, 1).start()
             ow_on(slot, 0).start()
 
     for k in range(records):
         o_pass(k).wait_recv()
         o_pass(k).start()
+
+    @pl.when(lead)
+    def _():
+        for t in range(3):
+            w_starts(t, 1)
+
+    for slot in range(records):
+
+        @pl.when(jnp.logical_not(ow_relays & (part == slot % parts)))
+        def _():
+            ow_on(slot, 0).wait_recv()
+
+            @pl.when(lead)
+            def _():
+                ow_on(slot, 0).start()
+
     for k in range(records):
         slot = k * parts + 1 - part
         remote(
@@ -554,6 +575,15 @@
     lax.fori_loop(0, cols // (2 * rows_here), project, 0)
     twin_lens.wait_recv()
     twin_gain.wait_recv()
+    shift_li.wait_recv()
+    width = og_here.shape[1]
+    for r in range(records):
+        inputs = li_here[:, r, :].astype(jnp.float32)
+        centered = inputs - jnp.sum(inputs, axis=1, keepdims=True) * (1.0 / width)
+        var = jnp.sum(centered * centered, axis=1, keepdims=True) * (1.0 / width)
+        deviation = 1.0 / jnp.sqrt(var + EPSILON)
+        normals[r] = centered * deviation
+        deviations[r] = jnp.broadcast_to(deviation, deviations.shape[1:])
     for t in range(3):
         for j in range(n):
             remote(
@@ -708,28 +738,21 @@
     lax.fori_loop(0, records, norm, 0)
 
     shift_og.wait_recv()
-    shift_li.wait_recv()
-    for src in range(records):
+
+    def finish(r):
+        rows = pl.ds(r * frames, frames)
+        normal = normals[r]
+        deviation = deviations[r][:, :1]
+        scaled = []
         for origin in range(records):
             remote(
                 sum_send.at[origin, 0],
-                part_recv.at[src, origin],
+                part_recv.at[r, origin],
                 p_send_sem.at[origin, 0],
-                p_recv_sem.at[src, origin],
+                p_recv_sem.at[r, origin],
                 before,
                 me,
             ).wait_recv()
-
-    width = og_here.shape[1]
-
-    def finish(r):
-        rows = pl.ds(r * frames, frames)
-        inputs = li_here[:, r, :].astype(jnp.float32)
-        centered = inputs - jnp.sum(inputs, axis=1, keepdims=True) * (1.0 / width)
-        var = jnp.sum(centered * centered, axis=1, keepdims=True) * (1.0 / width)
-        deviation = 1.0 / jnp.sqrt(var + EPSILON)
-        normal = centered * deviation
-        scaled = []
         for origin in range(records):
             scaled.append(part_recv[r, origin].astype(jnp.float32))
         scaled = jnp.concatenate(scaled, axis=1)
@@ -830,10 +853,6 @@
     w_rows = qkv_weight.shape[1]
     block = parts * w_rows
 
-    def by_record(x):
-        return x[0].transpose(1, 0, 2)
-
-    flat_grad = by_record(out_grad).reshape(records * frames, width)
     gain = norm_gain[0].reshape(records, 1, block)
     vmem = pl.BlockSpec(memory_space=pltpu.VMEM)
     low = jnp.bfloat16
@@ -841,9 +860,11 @@
     out = pl.pallas_call(
         functools.partial(body, (n, sections, records, parts, frames, cols)),
         out_shape=jax.ShapeDtypeStruct((records * frames, width), low),
-        in_specs=[pl.BlockSpec(memory_space=pltpu.SMEM)] + [vmem] * 8,
+        in_specs=[pl.BlockSpec(memory_space=pltpu.SMEM)] + [vmem] * 5 + [pl.BlockSpec(memory_space=pl.ANY)] * 2 + [vmem],
         out_specs=vmem,
-        scratch_shapes=[pltpu.VMEM((n, frames, cols), low)] * 3
+        scratch_shapes=[pltpu.VMEM((records, frames, features), low)] * 3
+        + [pltpu.VMEM((records * frames, width), low)]
+        + [pltpu.VMEM((n, frames, cols), low)] * 3
         + [
             pltpu.VMEM((n, frames, width), low),
             pltpu.VMEM((n * frames, cols), low),
@@ -857,6 +878,8 @@
             pltpu.VMEM((records, records, frames, block), low),
             pltpu.VMEM((frames, records, width), low),
             pltpu.VMEM((records * frames, width), low),
+            pltpu.VMEM((records, frames, width), jnp.float32),
+            pltpu.VMEM((records, frames, 128), jnp.float32),
             pltpu.VMEM((2, 8, 128), jnp.int32),
             pltpu.VMEM((records, 1, block), jnp.float32),
             dma((3, records, parts)),
@@ -887,10 +910,10 @@
     )(
         lengths[0],
         layer_input[0],
-        by_record(queries),
-        by_record(key_states),
-        by_record(value_states),
-        flat_grad,
+        queries[0],
+        key_states[0],
+        value_states[0],
+        out_grad[0],
         out_weight[0],
         qkv_weight[0],
         gain,

time: 150 us -> 144 us (0.960)
  local copies, waits for them, and re-layouts: 7.07 us -> 2.62 us
    transpose x2 -> x0, local copies, waits for them, and re-layouts: 2.31 us -> none  [by_record(): return x[0].transpose(1, 0, 2)]
    unnamed x7 -> x0, local copies, waits for them, and re-layouts: 2.14 us -> none
where the time goes in v3:
time: 144 us
  Pallas kernels  141 us (98%)
  local copies, waits for them, and re-layouts  2.62 us (2%)
    pallas_call x1, Pallas kernels, on_device_fused(): pl.pallas_call(functools.partial(body, (n, sections, records, parts, fram...  141 us

profile of v3, /device:TPU:27, one launch (start us, length us, event | category | flops | bytes accessed | tf_op | source)
XLA Modules:
  0.0 143.7 jit_solution(13171537564104130709)
XLA Ops:
  0.0 141.1 %shard_map.91 = bf16[256,1536]{1,0:T(8,128)(2,1)} custom-call(s32[4]{0:T(128)} %bitcast.24, bf16[64,4,1536]{2,1,0:T(4,128)(2,1)} %bitcast.17, bf16[64,4,1024]{2,1,0:T(4,128)(2,1)} %bitcast.19, bf16[64,4,1024]{2,1,0:T(4,128)(2,1)} %bitcast.20, bf16[64,4,1024]{2,1,0:T(4,128)(2,1)} %bitcast.21, bf16[64,4,1536]{2,1,0:T(4,128)(2,1)} %bitcast.18, ...), custom_call_target="tpu_custom_call" | custom-call | tf_op jit(solution)/shard_map/pallas_call | solution.py:860
  141.1 2.6 %copy.12 = bf16[4,64,1536]{2,0,1:T(4,128)(2,1)} copy(bf16[4,64,1536]{2,1,0:T(8,128)(2,1)} %bitcast.15) | data formatting | bytes 1572864 | tf_op jit(solution)/shard_map/reshape | solution.py:921

commit v4 on v3

--- a/solution.py
+++ b/solution.py
@@ -721,6 +721,9 @@
         def _():
             norm_send(last)
             w_pass(order(2), 2)
+
+        @pl.when(i == records - 1)
+        def _():
             w_pass(order(3), 2)
 
         norm_block(origin)

time: 144 us -> 141 us (0.979)
  Pallas kernels: 141 us -> 138 us
    pallas_call x1, Pallas kernels: 141 us -> 138 us  [on_device_fused(): pl.pallas_call(functools.partial(body, (n, sections, records, parts, fram...]
where the time goes in v4:
time: 141 us; the launch traced here: 140 us
  Pallas kernels  138 us (98%)
  local copies, waits for them, and re-layouts  2.62 us (2%)
    pallas_call x1, Pallas kernels, on_device_fused(): pl.pallas_call(functools.partial(body, (n, sections, records, parts, fram...  138 us

profile of v4, /device:TPU:27, one launch (start us, length us, event | category | flops | bytes accessed | tf_op | source)
XLA Modules:
  0.0 140.4 jit_solution(15657627349686274087)
XLA Ops:
  0.0 137.8 %shard_map.91 = bf16[256,1536]{1,0:T(8,128)(2,1)} custom-call(s32[4]{0:T(128)} %bitcast.24, bf16[64,4,1536]{2,1,0:T(4,128)(2,1)} %bitcast.17, bf16[64,4,1024]{2,1,0:T(4,128)(2,1)} %bitcast.19, bf16[64,4,1024]{2,1,0:T(4,128)(2,1)} %bitcast.20, bf16[64,4,1024]{2,1,0:T(4,128)(2,1)} %bitcast.21, bf16[64,4,1536]{2,1,0:T(4,128)(2,1)} %bitcast.18, ...), custom_call_target="tpu_custom_call" | custom-call | tf_op jit(solution)/shard_map/pallas_call | solution.py:863
  137.8 2.6 %copy.12 = bf16[4,64,1536]{2,0,1:T(4,128)(2,1)} copy(bf16[4,64,1536]{2,1,0:T(8,128)(2,1)} %bitcast.15) | data formatting | bytes 1572864 | tf_op jit(solution)/shard_map/reshape | solution.py:924
